TPU v7x, 256 devices: a whole 4x4x8 slice. The times are simulated.
256 devices in a mesh: pipe: 4 (over y_lo, core), ctx: 16 (over z, y_hi), tp: 4 (over x).
Axes of the slice: x: 4, y: 4 (y_hi: 2, y_lo: 2; y = y_hi * 2 + y_lo), z: 8, core: 2. Of those that a mesh axis runs over, the one named last changes fastest.
Arguments:
- segment_inputs: bfloat16 [4, 2, 2048, 4096], P('pipe', None, ('ctx', 'tp')), may hold values from -128 to 128
- keys: bfloat16 [4, 2, 2048, 512], P('pipe', None, 'ctx', 'tp'), may hold values from -64 to 64
- values: bfloat16 [4, 2, 2048, 512], P('pipe', None, 'ctx', 'tp'), may hold values from -6 to 6
- norm_gain: float32 [4, 4096], P('pipe'), may hold values from 0.1 to 1.9
- waiting_grads: bfloat16 [4, 2048, 4096], P('pipe', ('ctx', 'tp')), may hold values from -32 to 32
- output_grads: bfloat16 [1, 2048, 4096], P(None, ('ctx', 'tp')), may hold values from -32 to 32
- doc_lengths: int32 [5, 8], replicated, may hold values from 1 to 1024, as said below
Outputs:
- input_grads: bfloat16 [4, 2, 2048, 4096], P('pipe', None, ('ctx', 'tp'))
- key_grads: float32 [4, 2, 2048, 512], P('pipe', None, 'ctx', 'tp')
- value_grads: float32 [4, 2, 2048, 512], P('pipe', None, 'ctx', 'tp')
- gain_grads: float32 [4, 4096], P('pipe')
Inputs may be any that keep to these rules, and one draw needn't show every extreme that they name: `doc_lengths`: row m lists in order of position the lengths of the 8 documents packed into microbatch m's sequence; each row sums to 2048; the last document is exactly 1024 long.
All inputs are finite; a program needn't handle non-finite values.
Results may differ from a plain program's by a relative error of at most 0.009.
The roundings to bfloat16 on the way count: a program that leaves them out, or rounds other values in their place, can miss the bound.
Values may be sent and summed in bfloat16 or wider, within the bound.
A program may use at most 64 MiB of HBM per device.

v0:
```python
import jax
import jax.numpy as jnp
from jax import lax
from jax.sharding import PartitionSpec as P

HD = 128
S_DEV = 128
TICKS = 2
epsilon = 1e-05
masked_fill = -1e30


def passed_along(value, axis, by):
    count = lax.axis_size(axis)
    return lax.ppermute(value, axis, [(i, (i + by) % count) for i in range(count)])


def from_behind(value, axis, steps):
    count = lax.axis_size(axis)
    first, last = (max(0, -steps), min(count, count - steps))
    return lax.ppermute(value, axis, [(source, source + steps) for source in range(first, last)])


def row_positions(rows, half_rows, cycle_count):
    section = rows // half_rows
    offset = rows % half_rows
    owner = section // 2
    placed = jnp.where(section % 2 == 0, owner, 2 * cycle_count - 1 - owner)
    return placed * half_rows + offset


def document_starts(lengths_row, positions):
    closing = jnp.cumsum(lengths_row)
    passed = closing[None, :] <= positions[:, None]
    return jnp.sum(jnp.where(passed, lengths_row[None, :], 0), axis=1)


def keep_same(current):
    return current


def key_positions(key_first, key_count, cycle_count):
    rows = key_first + jnp.arange(key_count, dtype=jnp.int32)
    return row_positions(rows, S_DEV // 2, cycle_count)


def block_active(key_first, key_count, query_pos, query_start, cycle_count):
    key_pos = key_positions(key_first, key_count, cycle_count)
    return (jnp.min(key_pos) <= jnp.max(query_pos)) & (jnp.max(key_pos) >= jnp.min(query_start))


def score_block(query_block, key_block, query_pos, query_start, key_first, cycle_count):
    key_count = key_block.shape[0]
    key_pos = key_positions(key_first, key_count, cycle_count)
    scores = HD ** (-0.5) * jnp.einsum(
        "rkgd,skd->kgrs", query_block, key_block, preferred_element_type=jnp.float32
    )
    visible = (key_pos[None, :] <= query_pos[:, None]) & (key_pos[None, :] >= query_start[:, None])
    return (scores, visible[None, None])


def forward_update(carry, key_flat, value_flat, key_first, context):
    query_block, grad_block, query_pos, query_start, cycle_count = context
    key_count = key_flat.shape[0]

    def apply_block(current):
        row_peak, row_total, weighted = current
        key_block = key_flat.reshape(key_count, -1, HD)
        value_block = value_flat.reshape(key_count, -1, HD)
        scores, visible = score_block(
            query_block, key_block, query_pos, query_start, key_first, cycle_count
        )
        block_peak = jnp.max(jnp.where(visible, scores, masked_fill), axis=-1)
        new_peak = jnp.maximum(row_peak, block_peak)
        weights = jnp.where(visible, jnp.exp(scores - new_peak[..., None]), 0.0)
        prob_grad = jnp.einsum(
            "rkgd,skd->kgrs", grad_block, value_block, preferred_element_type=jnp.float32
        )
        return (new_peak, jnp.sum(weights, axis=-1), jnp.sum(weights * prob_grad, axis=-1))

    return lax.cond(
        block_active(key_first, key_count, query_pos, query_start, cycle_count),
        apply_block,
        keep_same,
        carry,
    )


def backward_terms(key_flat, value_flat, key_first, context, row_stats):
    query_block, grad_block, query_pos, query_start, cycle_count = context
    logsum, row_term = row_stats
    key_count = key_flat.shape[0]
    key_block = key_flat.reshape(key_count, -1, HD)
    value_block = value_flat.reshape(key_count, -1, HD)
    scale_factor = HD ** (-0.5)
    scores, visible = score_block(
        query_block, key_block, query_pos, query_start, key_first, cycle_count
    )
    prob_weights = jnp.where(visible, jnp.exp(scores - logsum[..., None]), 0.0)
    prob_grad = jnp.einsum(
        "rkgd,skd->kgrs", grad_block, value_block, preferred_element_type=jnp.float32
    )
    dscore = (prob_weights * (prob_grad - row_term[..., None])).astype(jnp.bfloat16)
    probs_low = prob_weights.astype(jnp.bfloat16)
    query_add = scale_factor * jnp.einsum(
        "kgrs,skd->rkgd", dscore, key_block, preferred_element_type=jnp.float32
    )
    key_add = scale_factor * jnp.einsum(
        "kgrs,rkgd->skd", dscore, query_block, preferred_element_type=jnp.float32
    )
    value_add = jnp.einsum(
        "kgrs,rkgd->skd", probs_low, grad_block, preferred_element_type=jnp.float32
    )
    return (query_add, key_add.reshape(key_count, -1), value_add.reshape(key_count, -1))


def segment_tick(inputs, key_local, value_local, gain_row, arriving, lengths_row):
    widened = inputs.astype(jnp.float32)
    inverse = lax.rsqrt(jnp.mean(widened * widened, axis=-1, keepdims=True) + epsilon)
    normed = widened * inverse
    queries = (normed * gain_row[None, :]).astype(jnp.bfloat16)
    query_heads, grad_heads = (
        lax.all_to_all(queries, "tp", split_axis=1, concat_axis=0, tiled=True),
        lax.all_to_all(arriving, "tp", split_axis=1, concat_axis=0, tiled=True),
    )
    row_count = key_local.shape[0]
    kv_local = key_local.shape[1] // HD
    group_size = query_heads.shape[1] // (HD * kv_local)
    query_block = query_heads.reshape(row_count, kv_local, group_size, HD)
    grad_block = grad_heads.reshape(row_count, kv_local, group_size, HD)
    cycle_count = lax.axis_size("ctx")
    cycle_place = lax.axis_index("ctx")
    query_pos = key_positions(cycle_place * row_count, row_count, cycle_count)
    query_start = document_starts(lengths_row, query_pos)
    context = (query_block, grad_block, query_pos, query_start, cycle_count)
    empty_peak = jnp.full((kv_local, group_size, row_count), masked_fill, jnp.float32)
    zero_rows = jnp.zeros((kv_local, group_size, row_count), jnp.float32)
    initial = (empty_peak, zero_rows, zero_rows)
    row_peak, row_total, weighted = forward_update(
        initial,
        lax.all_gather(key_local, "ctx", axis=0, tiled=True),
        lax.all_gather(value_local, "ctx", axis=0, tiled=True),
        jnp.int32(0),
        context,
    )
    row_stats = (row_peak + jnp.log(row_total), weighted / row_total)
    query_zero = jnp.zeros((row_count, kv_local, group_size, HD), jnp.float32)

    def cycle_turn(cycle_step, carry):
        key_block, value_block, key_grad, value_grad, query_grad = carry
        owner_index = (cycle_place - cycle_step) % cycle_count
        block_first = owner_index * row_count

        def apply_terms(current):
            added_terms = backward_terms(key_block, value_block, block_first, context, row_stats)
            return (
                current[0] + added_terms[1],
                current[1] + added_terms[2],
                current[2] + added_terms[0],
            )

        key_grad, value_grad, query_grad = lax.cond(
            block_active(block_first, row_count, query_pos, query_start, cycle_count),
            apply_terms,
            keep_same,
            (key_grad, value_grad, query_grad),
        )
        key_block, value_block = passed_along((key_block, value_block), "ctx", 1)
        key_grad, value_grad = passed_along((key_grad, value_grad), "ctx", 1)
        return (key_block, value_block, key_grad, value_grad, query_grad)

    zero_kv = jnp.zeros(key_local.shape, jnp.float32)
    finished = lax.fori_loop(
        0, cycle_count, cycle_turn, (key_local, value_local, zero_kv, zero_kv, query_zero)
    )
    key_grad, value_grad, query_grad = (finished[2], finished[3], finished[4])
    query_low = query_grad.reshape(row_count, -1).astype(jnp.bfloat16)
    grad_rows = lax.all_to_all(query_low, "tp", split_axis=0, concat_axis=1, tiled=True)
    rounded = grad_rows.astype(jnp.float32)
    scaled = rounded * gain_row[None, :]
    coupling = jnp.mean(scaled * normed, axis=-1, keepdims=True)
    input_grad = (arriving.astype(jnp.float32) + inverse * (scaled - normed * coupling)).astype(
        jnp.bfloat16
    )
    gain_part = jnp.sum(rounded * normed, axis=0)
    return (input_grad, key_grad, value_grad, gain_part)


def on_device(segment_inputs, keys, values, norm_gain, waiting_grads, output_grads, doc_lengths):
    segment_index = lax.axis_index("pipe")
    last_segment = lax.axis_size("pipe") - 1
    gain_row = norm_gain[0]
    arriving = waiting_grads[0]
    input_list = []
    key_list = []
    value_list = []
    gain_running = jnp.zeros(gain_row.shape, jnp.float32)
    for tick_index in range(TICKS):
        micro_index = segment_index + tick_index
        lengths_row = lax.dynamic_index_in_dim(doc_lengths, micro_index, 0, keepdims=False)
        input_grad, key_grad, value_grad, gain_part = segment_tick(
            segment_inputs[0, tick_index],
            keys[0, tick_index],
            values[0, tick_index],
            gain_row,
            arriving,
            lengths_row,
        )
        input_list.append(input_grad)
        key_list.append(key_grad)
        value_list.append(value_grad)
        gain_running = gain_running + gain_part
        if tick_index + 1 < TICKS:
            arrived = from_behind(input_grad, "pipe", -1)
            arriving = jnp.where(segment_index == last_segment, output_grads[tick_index], arrived)
    gain_grads = lax.psum(gain_running, ("ctx", "tp"))
    return (
        jnp.stack(input_list)[None],
        jnp.stack(key_list)[None],
        jnp.stack(value_list)[None],
        gain_grads[None],
    )


def solution(mesh):
    in_specs = (
        P("pipe", None, ("ctx", "tp"), None),
        P("pipe", None, "ctx", "tp"),
        P("pipe", None, "ctx", "tp"),
        P("pipe", None),
        P("pipe", ("ctx", "tp"), None),
        P(None, ("ctx", "tp"), None),
        P(),
    )
    out_specs = (
        P("pipe", None, ("ctx", "tp"), None),
        P("pipe", None, "ctx", "tp"),
        P("pipe", None, "ctx", "tp"),
        P("pipe", None),
    )
    return jax.shard_map(
        on_device, mesh=mesh, in_specs=in_specs, out_specs=out_specs, check_vma=False
    )
```

profile of v0, /device:TPU:8, one launch (start us, length us, event | category | flops | bytes accessed | tf_op | source)
XLA Modules:
  0.0 1165.9 jit_solution(12238675916187327474)
XLA Ops:
  6.3 4.3 all-to-all-start
  21.4 46.2 %all-gather = bf16[1,1,2048,128]{3,2,1,0:T(8,128)(2,1)S(1)} all-gather(bf16[1,1,128,128]{3,2,1,0:T(8,128)(2,1)S(1)} %get-tuple-element.1508), channel_id=2, replica_groups=mesh['pipe'=4,'ctx'=16,'tp'=4] {'ctx'}, dimensions={2}, use_global_device_ids=true | all-gather | bytes 557056 | tf_op jit(solution)/shard_map/all_gather | solution.py:141
  67.7 4.5 all-to-all-start.1
  72.2 40.6 %all-gather.1 = bf16[1,1,2048,128]{3,2,1,0:T(8,128)(2,1)} all-gather(bf16[1,1,128,128]{3,2,1,0:T(8,128)(2,1)S(1)} %get-tuple-element.1495), channel_id=3, replica_groups=mesh['pipe'=4,'ctx'=16,'tp'=4] {'ctx'}, dimensions={2}, use_global_device_ids=true | all-gather | bytes 557056 | tf_op jit(solution)/shard_map/all_gather | solution.py:142
  113.0 6.8 conditional.4
  120.0 273.9 %while.50 = (s32[]{:T(128)}, bf16[128,128]{1,0:T(8,128)(2,1)S(1)}, bf16[128,128]{1,0:T(8,128)(2,1)S(1)}, f32[128,128]{1,0:T(8,128)S(1)}, f32[128,128]{1,0:T(8,12...) while((s32[]{:T(128)}, bf16[128,128]{1,0:T(8,128)(2,1)S(1)}, ...), condition=%wide.region_17.18_spmd.clone, body=%wide.region_12.17_spmd.clone.sunk | while | flops 169071120 | bytes 6050608 | solution.py:173
  124.7 3.7 collective-permute-start.2
  133.1 3.2 collective-permute-done.3
  145.4 4.3 collective-permute-start.1
  159.8 3.5 collective-permute-start.3
  167.7 3.1 collective-permute-done
  182.6 3.1 collective-permute-done.2
  192.8 3.3 collective-permute-start.3
  198.5 3.0 collective-permute-start.1
  211.9 4.9 collective-permute-start.3
  219.8 4.8 collective-permute-done
  233.5 4.1 collective-permute-done.2
  245.1 3.3 collective-permute-start.3
  249.4 4.5 collective-permute-start.1
  264.2 2.7 collective-permute-start.3
  282.3 4.7 collective-permute-start.1
  297.2 2.9 collective-permute-start.3
  302.6 2.8 collective-permute-start.1
  315.6 2.8 collective-permute-start.3
  334.3 3.1 collective-permute-start.1
  347.7 4.5 collective-permute-start.3
  352.7 2.8 collective-permute-start.1
  355.6 4.1 collective-permute-done
  381.0 4.3 collective-permute-start.3
  386.3 4.7 collective-permute-start.1
  394.9 5.4 all-to-all-start.2
  400.3 6.7 all-to-all-done.2
  411.5 41.4 %all-gather.2 = bf16[1,1,2048,128]{3,2,1,0:T(8,128)(2,1)S(1)} all-gather(bf16[1,1,128,128]{3,2,1,0:T(8,128)(2,1)S(1)} %get-tuple-element.1505), channel_id=4, replica_groups=mesh['pipe'=4,'ctx'=16,'tp'=4] {'ctx'}, dimensions={2}, use_global_device_ids=true | all-gather | bytes 557056 | tf_op jit(solution)/shard_map/all_gather | solution.py:141
  454.9 41.8 %all-gather.3 = bf16[1,1,2048,128]{3,2,1,0:T(8,128)(2,1)} all-gather(bf16[1,1,128,128]{3,2,1,0:T(8,128)(2,1)S(1)} %get-tuple-element.1492), channel_id=5, replica_groups=mesh['pipe'=4,'ctx'=16,'tp'=4] {'ctx'}, dimensions={2}, use_global_device_ids=true | all-gather | bytes 557056 | tf_op jit(solution)/shard_map/all_gather | solution.py:142
  496.7 3.4 all-to-all-start.3
  502.7 4.1 all-to-all-done.3
  506.8 4.0 all-to-all-start.4
  512.4 5.1 all-to-all-done.4
  518.6 6.9 conditional.5
  525.6 273.6 %while.51 = (s32[]{:T(128)}, bf16[128,128]{1,0:T(8,128)(2,1)S(1)}, bf16[128,128]{1,0:T(8,128)(2,1)S(1)}, f32[128,128]{1,0:T(8,128)S(1)}, f32[128,128]{1,0:T(8,12...) while((s32[]{:T(128)}, bf16[128,128]{1,0:T(8,128)(2,1)S(1)}, ...), condition=%wide.region_33.34_spmd.clone, body=%wide.region_28.33_spmd.clone.sunk | while | flops 169071120 | bytes 6050608 | solution.py:173
  535.4 3.6 collective-permute-done.6
  550.4 4.7 collective-permute-start.5
  562.7 2.7 collective-permute-start.6
  567.5 3.6 collective-permute-start.4
  575.0 3.6 collective-permute-done.5
  587.4 3.9 collective-permute-done.6
  603.3 3.1 collective-permute-start.5
  616.8 4.9 collective-permute-start.7
  624.7 4.5 collective-permute-done.4
  638.8 3.5 collective-permute-done.6
  650.0 4.1 collective-permute-start.7
  655.0 4.7 collective-permute-start.5
  667.4 2.7 collective-permute-start.6
  670.0 2.6 collective-permute-start.7
  688.3 3.7 collective-permute-start.5
  702.3 3.1 collective-permute-start.7
  740.2 3.1 collective-permute-start.5
  753.7 4.9 collective-permute-start.7
  761.6 4.5 collective-permute-done.4
  786.8 3.7 collective-permute-start.7
  791.7 4.7 collective-permute-start.5
  800.3 3.4 all-to-all-start.5
  805.0 5.3 all-to-all-done.5
  810.8 353.9 %psum.7 = f32[1,4096]{1,0:T(1,128)} all-reduce(f32[1,4096]{1,0:T(1,128)S(1)} %bitcast.426), channel_id=1, replica_groups=mesh['pipe'=4,'ctx'=16,'tp'=4] {'ctx','tp'}, use_global_device_ids=true, to_apply=%region_37.38 | all-reduce | flops 4096 | bytes 32768 | tf_op jit(solution)/shard_map/psum | solution.py:216
  (956 shorter events, 382.2 us)
Async XLA Ops:
  6.3 61.3 %all-to-all-start = ((bf16[32,4,1024]{2,0,1:T(8,128)(2,1)}), bf16[32,4,1024]{2,0,1:T(8,128)(2,1)S(1)}, u32[]{:S(2)}, u32[]{:S(2)}) async-start(bf16[32,4,1024]{2,0,1:T(8,128)(2,1)} %multiply_convert_fusion.1), calls=%async_computation | async-start | bytes 524288 | tf_op jit(solution)/shard_map/all_to_all | solution.py:123
  67.7 45.2 %all-to-all-start.1 = ((bf16[32,4,1024]{2,0,1:T(8,128)(2,1)}), bf16[32,4,1024]{2,0,1:T(8,128)(2,1)S(1)}, u32[]{:S(2)}, u32[]{:S(2)}) async-start(bf16[32,4,1024]{2,0,1:T(8,128)(2,1)} %copy.84), calls=%async_computation.1 | async-start | bytes 524288 | tf_op jit(solution)/shard_map/all_to_all | solution.py:124
  124.7 8.4 collective-permute-start.2
  128.6 8.2 collective-permute-start
  143.0 8.3 collective-permute-start.2
  143.1 9.3 collective-permute-start.3
  144.4 8.3 collective-permute-start
  157.8 9.0 collective-permute-start.2
  177.7 8.0 collective-permute-start.2
  177.8 8.6 collective-permute-start.3
  192.7 8.8 collective-permute-start.2
  192.8 8.7 collective-permute-start.3
  210.7 8.1 collective-permute-start.2
  216.8 8.1 collective-permute-start.1
  229.7 8.0 collective-permute-start.2
  229.7 8.7 collective-permute-start.3
  232.2 8.1 collective-permute-start.1
  245.0 9.0 collective-permute-start.2
  245.1 8.9 collective-permute-start.3
  261.7 8.4 collective-permute-start.2
  267.0 8.1 collective-permute-start.1
  279.8 8.6 collective-permute-start.2
  279.8 9.8 collective-permute-start.3
  281.5 8.5 collective-permute-start
  282.3 8.0 collective-permute-start.1
  295.0 10.4 collective-permute-start.2
  297.2 8.2 collective-permute-start.3
  331.1 8.6 collective-permute-start.3
  346.5 9.0 collective-permute-start.2
  380.8 10.3 collective-permute-start.2
  381.0 10.1 collective-permute-start.3
  394.9 12.0 %all-to-all-start.2 = ((bf16[4,32,1024]{2,1,0:T(8,128)(2,1)}), bf16[4,32,1024]{2,1,0:T(8,128)(2,1)S(1)}, u32[]{:S(2)}, u32[]{:S(2)}) async-start(bf16[4,32,1024]{2,1,0:T(8,128)(2,1)} %convert_element_type.172), calls=%async_computation.2 | async-start | bytes 524288 | tf_op jit(solution)/shard_map/all_to_all | solution.py:178
  409.6 91.3 %collective-permute-start.8 = (bf16[32,4096]{1,0:T(8,128)(2,1)}, bf16[32,4096]{1,0:T(8,128)(2,1)}, u32[]{:S(2)}, u32[]{:S(2)}) collective-permute-start(bf16[32,4096]{1,0:T(8,128)(2,1)} %fusion.122), channel_id=1, source_target_pairs={{64,0},{128,64},{192,128},{65,1},{129,65},{193,129},{66,2},{130,66... | collective-permute-start | bytes 786440 | tf_op jit(solution)/shard_map/ppermute | solution.py:21
  496.7 10.1 all-to-all-start.3
  506.8 10.8 all-to-all-start.4
  530.4 8.6 collective-permute-start.6
  533.1 8.1 collective-permute-start.4
  547.6 8.1 collective-permute-start.6
  547.7 8.7 collective-permute-start.7
  562.7 9.6 collective-permute-start.6
  583.4 8.6 collective-permute-start.7
  598.3 8.1 collective-permute-start.6
  598.4 8.6 collective-permute-start.7
  615.6 8.7 collective-permute-start.6
  634.6 8.5 collective-permute-start.7
  636.8 8.3 collective-permute-start.5
  649.9 9.8 collective-permute-start.6
  650.0 9.8 collective-permute-start.7
  667.4 8.1 collective-permute-start.6
  670.0 8.0 collective-permute-start.7
  685.3 8.3 collective-permute-start.6
  685.4 8.9 collective-permute-start.7
  700.6 9.8 collective-permute-start.6
  702.3 8.1 collective-permute-start.7
  720.2 8.0 collective-permute-start.6
  720.6 8.2 collective-permute-start.7
  735.9 8.0 collective-permute-start.6
  736.2 8.4 collective-permute-start.7
  752.5 8.8 collective-permute-start.6
  771.2 8.0 collective-permute-start.6
  771.6 8.3 collective-permute-start.7
  786.7 9.7 collective-permute-start.6
  786.8 9.6 collective-permute-start.7
  800.3 10.1 all-to-all-start.5
  (82 other events, 3647.2 us)
where the time goes:
time: 1170 us
  blocking collectives  524 us (45%)
  starting transfers between devices  263 us (22%)
  waiting for transfers between devices  180 us (15%)
  loops' own time  85 us (7%)
  other arithmetic  51.5 us (4%)
  matrix products  46.7 us (4%)
    psum x1, blocking collectives, on_device(): gain_grads = lax.psum(gain_running, ('ctx', 'tp'))  354 us
    ppermute x128, starting transfers between devices, passed_along(): lax.ppermute(value, axis, [(i, (i + by) % count) for i in range(count)])  236 us
    ppermute x128, waiting for transfers between devices, passed_along(): lax.ppermute(value, axis, [(i, (i + by) % count) for i in range(count)])  159 us
    all_gather x2, blocking collectives, segment_tick(): lax.all_gather(key_local, 'ctx', axis=0, tiled=True)  87.6 us
    all_gather x2, blocking collectives, segment_tick(): lax.all_gather(value_local, 'ctx', axis=0, tiled=True)  82.4 us
    another operation x2, loops' own time, segment_tick(): lax.fori_loop(0, cycle_count, cycle_turn, (key_local, value_local, zero_k...  82.4 us
    reduce_max x33, other arithmetic, block_active(): jnp.max(key_pos) >= jnp.min(query_start)  23.7 us
  transfers between devices with their start and end apart: 135, of which 110 were waited for; matrix products, arithmetic and copies ran while one was open for 1% of the time, Pallas kernels for 0%

commit v1 on v0

--- a/solution.py
+++ b/solution.py
@@ -213,7 +213,7 @@
         if tick_index + 1 < TICKS:
             arrived = from_behind(input_grad, "pipe", -1)
             arriving = jnp.where(segment_index == last_segment, output_grads[tick_index], arrived)
-    gain_grads = lax.psum(gain_running, ("ctx", "tp"))
+    gain_grads = jnp.sum(lax.all_gather(gain_running, ("ctx", "tp")), axis=0)
     return (
         jnp.stack(input_list)[None],
         jnp.stack(key_list)[None],

time: 1170 us -> 1000 us (0.85)
  blocking collectives: 524 us -> 170 us
  waiting for transfers between devices: 180 us -> 272 us
  local copies, waits for them, and re-layouts: 10.6 us -> 50.3 us
  matrix products: 46.7 us -> 68.6 us
  other arithmetic: 51.5 us -> 65.8 us
  between operations: 4.94 us -> 18.2 us
    psum x1 -> x0, blocking collectives: 354 us -> none  [on_device(): gain_grads = lax.psum(gain_running, ('ctx', 'tp'))]
    all_gather x0 -> x1, waiting for transfers between devices: none -> 107 us  [on_device(): gain_grads = jnp.sum(lax.all_gather(gain_running, ('ctx', 'tp')), axis=0)]
    while x128, local copies, waits for them, and re-layouts: 0.61 us -> 38.1 us
  transfers between devices with their start and end apart: 135 -> 136, of which waited for: 110 -> 103; matrix products, arithmetic and copies ran while one was open for 1% -> 3% of each run, Pallas kernels for 0% -> 0%
where the time goes in v1:
time: 1000 us; the launch traced here: 992 us
  waiting for transfers between devices  272 us (27%)
  starting transfers between devices  264 us (26%)
  blocking collectives  170 us (17%)
  loops' own time  83.7 us (8%)
  matrix products  68.6 us (7%)
  other arithmetic  65.8 us (7%)
  local copies, waits for them, and re-layouts  50.3 us (5%)
  between operations  18.2 us (2%)
    ppermute x128, starting transfers between devices, passed_along(): lax.ppermute(value, axis, [(i, (i + by) % count) for i in range(count)])  235 us
    ppermute x128, waiting for transfers between devices, passed_along(): lax.ppermute(value, axis, [(i, (i + by) % count) for i in range(count)])  148 us
    all_gather x1, waiting for transfers between devices, on_device(): gain_grads = jnp.sum(lax.all_gather(gain_running, ('ctx', 'tp')), axis=0)  107 us
    all_gather x2, blocking collectives, segment_tick(): lax.all_gather(key_local, 'ctx', axis=0, tiled=True)  87.5 us
    all_gather x2, blocking collectives, segment_tick(): lax.all_gather(value_local, 'ctx', axis=0, tiled=True)  82.4 us
    another operation x2, loops' own time, segment_tick(): lax.fori_loop(0, cycle_count, cycle_turn, (key_local, value_local, zero_k...  81.1 us
    while x128, local copies, waits for them, and re-layouts  38.1 us
    reduce_max x33, other arithmetic, block_active(): jnp.max(key_pos) >= jnp.min(query_start)  23.1 us
  transfers between devices with their start and end apart: 136, of which 103 were waited for; matrix products, arithmetic and copies ran while one was open for 3% of the time, Pallas kernels for 0%

profile of v1, /device:TPU:8, one launch (start us, length us, event | category | flops | bytes accessed | tf_op | source)
XLA Modules:
  0.0 992.2 jit_solution(16721649081407660619)
XLA Ops:
  12.8 4.3 all-to-all-start
  28.4 46.2 %all-gather = bf16[1,1,2048,128]{3,2,1,0:T(8,128)(2,1)S(1)} all-gather(bf16[1,1,128,128]{3,2,1,0:T(8,128)(2,1)S(1)} %get-tuple-element.1508), channel_id=2, replica_groups=mesh['pipe'=4,'ctx'=16,'tp'=4] {'ctx'}, dimensions={2}, use_global_device_ids=true | all-gather | bytes 557056 | tf_op jit(solution)/shard_map/all_gather | solution.py:141
  74.6 4.5 all-to-all-start.1
  79.1 40.6 %all-gather.1 = bf16[1,1,2048,128]{3,2,1,0:T(8,128)(2,1)} all-gather(bf16[1,1,128,128]{3,2,1,0:T(8,128)(2,1)S(1)} %get-tuple-element.1495), channel_id=3, replica_groups=mesh['pipe'=4,'ctx'=16,'tp'=4] {'ctx'}, dimensions={2}, use_global_device_ids=true | all-gather | bytes 557056 | tf_op jit(solution)/shard_map/all_gather | solution.py:142
  120.0 6.8 conditional.4
  127.0 273.8 %while.50 = (s32[]{:T(128)}, bf16[128,128]{1,0:T(8,128)(2,1)S(1)}, bf16[128,128]{1,0:T(8,128)(2,1)S(1)}, f32[128,128]{1,0:T(8,128)S(1)}, f32[128,128]{1,0:T(8,12...) while((s32[]{:T(128)}, bf16[128,128]{1,0:T(8,128)(2,1)S(1)}, ...), condition=%wide.region_17.18_spmd.clone, body=%wide.region_12.17_spmd.clone.sunk | while | flops 169071120 | bytes 6050608 | solution.py:173
  131.7 3.7 collective-permute-start.2
  140.1 3.2 collective-permute-done.3
  152.3 4.3 collective-permute-start.1
  166.8 3.5 collective-permute-start.3
  174.7 3.1 collective-permute-done
  189.5 3.1 collective-permute-done.2
  199.7 3.3 collective-permute-start.3
  205.4 3.1 collective-permute-start.1
  218.8 4.9 collective-permute-start.3
  226.7 4.8 collective-permute-done
  240.4 4.1 collective-permute-done.2
  252.2 3.1 collective-permute-start.3
  256.5 4.4 collective-permute-start.1
  289.2 4.7 collective-permute-start.1
  341.2 3.3 collective-permute-start.1
  354.6 4.4 collective-permute-start.3
  362.5 4.1 collective-permute-done
  387.8 4.2 collective-permute-start.3
  393.2 4.7 collective-permute-start.1
  401.8 5.3 all-to-all-start.2
  407.1 6.7 all-to-all-done.2
  420.1 41.3 %all-gather.2 = bf16[1,1,2048,128]{3,2,1,0:T(8,128)(2,1)S(1)} all-gather(bf16[1,1,128,128]{3,2,1,0:T(8,128)(2,1)S(1)} %get-tuple-element.1505), channel_id=4, replica_groups=mesh['pipe'=4,'ctx'=16,'tp'=4] {'ctx'}, dimensions={2}, use_global_device_ids=true | all-gather | bytes 557056 | tf_op jit(solution)/shard_map/all_gather | solution.py:141
  461.3 3.4 all-to-all-start.3
  466.5 4.9 all-to-all-done.3
  471.4 4.0 all-to-all-start.4
  475.5 41.7 %all-gather.3 = bf16[1,1,2048,128]{3,2,1,0:T(8,128)(2,1)} all-gather(bf16[1,1,128,128]{3,2,1,0:T(8,128)(2,1)S(1)} %get-tuple-element.1492), channel_id=5, replica_groups=mesh['pipe'=4,'ctx'=16,'tp'=4] {'ctx'}, dimensions={2}, use_global_device_ids=true | all-gather | bytes 557056 | tf_op jit(solution)/shard_map/all_gather | solution.py:142
  520.0 6.9 conditional.5
  527.6 330.0 %while.51 = (s32[]{:T(128)}, bf16[128,128]{1,0:T(8,128)(2,1)}, bf16[128,128]{1,0:T(8,128)(2,1)}, f32[128,128]{1,0:T(8,128)S(1)}, f32[128,128]{1,0:T(8,128)S(1)},...) while((s32[]{:T(128)}, bf16[128,128]{1,0:T(8,128)(2,1)}, ...), condition=%wide.region_33.34_spmd.clone, body=%wide.region_28.33_spmd.clone.sunk | while | flops 169071120 | bytes 6050608 | solution.py:173
  532.4 3.4 conditional.11
  553.8 3.4 conditional.11
  558.6 4.7 collective-permute-start.5
  572.5 3.4 conditional.11
  595.2 3.4 conditional.11
  603.7 3.3 collective-permute-done.6
  614.5 3.4 conditional.11
  635.9 3.4 conditional.11
  639.9 4.8 collective-permute-start.7
  648.3 4.1 collective-permute-done.4
  657.5 3.4 conditional.11
  676.4 3.4 conditional.11
  680.0 3.4 collective-permute-start.7
  683.9 4.8 collective-permute-start.5
  696.3 3.4 conditional.11
  717.8 3.4 conditional.11
  724.9 4.6 collective-permute-start.5
  737.3 3.4 conditional.11
  761.1 3.4 conditional.11
  780.7 3.4 conditional.11
  800.4 3.4 conditional.11
  804.1 4.7 collective-permute-start.7
  821.9 3.4 conditional.11
  825.5 3.4 collective-permute-start.7
  842.0 3.4 conditional.11
  845.5 4.1 collective-permute-start.7
  850.0 4.7 collective-permute-start.5
  858.6 4.9 all-to-all-start.5
  864.3 5.8 all-to-all-done.5
  875.9 106.7 %all-gather.7.cloned.1.call-done = f32[64,1,4096]{2,1,0:T(1,128)} async-done(((f32[1,1,4096]{2,1,0:T(1,128)}), f32[64,1,4096]{2,1,0:T(1,128)}) %all-gather.7.cloned.1.call-update) | async-done | bytes 1048592 | tf_op jit(solution)/shard_map/all_gather | solution.py:216
  (961 shorter events, 471.5 us)
Async XLA Ops:
  12.8 61.8 %all-to-all-start = ((bf16[32,4,1024]{2,0,1:T(8,128)(2,1)}), bf16[32,4,1024]{2,0,1:T(8,128)(2,1)S(1)}, u32[]{:S(2)}, u32[]{:S(2)}) async-start(bf16[32,4,1024]{2,0,1:T(8,128)(2,1)} %multiply_convert_fusion.1), calls=%async_computation | async-start | bytes 524288 | tf_op jit(solution)/shard_map/all_to_all | solution.py:123
  74.6 45.2 %all-to-all-start.1 = ((bf16[32,4,1024]{2,0,1:T(8,128)(2,1)}), bf16[32,4,1024]{2,0,1:T(8,128)(2,1)S(1)}, u32[]{:S(2)}, u32[]{:S(2)}) async-start(bf16[32,4,1024]{2,0,1:T(8,128)(2,1)} %copy.84), calls=%async_computation.1 | async-start | bytes 524288 | tf_op jit(solution)/shard_map/all_to_all | solution.py:124
  131.7 8.4 collective-permute-start.2
  135.5 8.2 collective-permute-start
  149.9 8.3 collective-permute-start.2
  150.0 9.3 collective-permute-start.3
  151.3 8.3 collective-permute-start
  164.7 9.0 collective-permute-start.2
  184.8 8.6 collective-permute-start.3
  199.7 8.8 collective-permute-start.2
  199.7 8.8 collective-permute-start.3
  217.7 8.1 collective-permute-start.2
  236.6 8.7 collective-permute-start.3
  239.1 8.3 collective-permute-start.1
  252.1 8.8 collective-permute-start.2
  252.2 9.0 collective-permute-start.3
  268.7 8.2 collective-permute-start.2
  273.9 8.1 collective-permute-start.1
  286.7 8.6 collective-permute-start.2
  286.8 9.8 collective-permute-start.3
  288.4 8.5 collective-permute-start
  301.9 10.4 %collective-permute-start.2 = (f32[128,128]{1,0:T(8,128)S(1)}, f32[128,128]{1,0:T(8,128)S(1)}, u32[]{:S(2)}, u32[]{:S(2)}) collective-permute-start(f32[128,128]{1,0:T(8,128)S(1)} %get-tuple-element.1700), channel_id=1, source_target_pairs={{0,4},{4,8},{8,12},{12,16},{16,20},{20,24},{24,28},{28,32},{32,36}... | collective-permute-start | bytes 196616 | tf_op jit(solution)/shard_map/while/body/eval_jaxpr/ppermute | solution.py:15
  304.1 8.2 collective-permute-start.3
  353.4 9.0 collective-permute-start.2
  387.6 10.3 %collective-permute-start.2 = (f32[128,128]{1,0:T(8,128)S(1)}, f32[128,128]{1,0:T(8,128)S(1)}, u32[]{:S(2)}, u32[]{:S(2)}) collective-permute-start(f32[128,128]{1,0:T(8,128)S(1)} %get-tuple-element.1700), channel_id=1, source_target_pairs={{0,4},{4,8},{8,12},{12,16},{16,20},{20,24},{24,28},{28,32},{32,36}... | collective-permute-start | bytes 196616 | tf_op jit(solution)/shard_map/while/body/eval_jaxpr/ppermute | solution.py:15
  387.8 10.1 %collective-permute-start.3 = (f32[128,128]{1,0:T(8,128)S(1)}, f32[128,128]{1,0:T(8,128)S(1)}, u32[]{:S(2)}, u32[]{:S(2)}) collective-permute-start(f32[128,128]{1,0:T(8,128)S(1)} %get-tuple-element.1701), channel_id=1, source_target_pairs={{0,4},{4,8},{8,12},{12,16},{16,20},{20,24},{24,28},{28,32},{32,36}... | collective-permute-start | bytes 196616 | tf_op jit(solution)/shard_map/while/body/eval_jaxpr/ppermute | solution.py:15
  401.8 12.0 %all-to-all-start.2 = ((bf16[4,32,1024]{2,1,0:T(8,128)(2,1)}), bf16[4,32,1024]{2,1,0:T(8,128)(2,1)S(1)}, u32[]{:S(2)}, u32[]{:S(2)}) async-start(bf16[4,32,1024]{2,1,0:T(8,128)(2,1)} %convert_element_type.172), calls=%async_computation.2 | async-start | bytes 524288 | tf_op jit(solution)/shard_map/all_to_all | solution.py:178
  416.2 48.6 %collective-permute-start.8 = (bf16[32,4096]{1,0:T(8,128)(2,1)S(1)}, bf16[32,4096]{1,0:T(8,128)(2,1)S(1)}, u32[]{:S(2)}, u32[]{:S(2)}) collective-permute-start(bf16[32,4096]{1,0:T(8,128)(2,1)S(1)} %fusion.122), channel_id=1, source_target_pairs={{64,0},{128,64},{192,128},{65,1},{129,65},{193,129},{66,2},{130,66... | collective-permute-start | bytes 786440 | tf_op jit(solution)/shard_map/ppermute | solution.py:21
  461.3 10.1 %all-to-all-start.3 = ((bf16[32,4,1024]{2,0,1:T(8,128)(2,1)}), bf16[32,4,1024]{2,0,1:T(8,128)(2,1)S(1)}, u32[]{:S(2)}, u32[]{:S(2)}) async-start(bf16[32,4,1024]{2,0,1:T(8,128)(2,1)} %get-tuple-element.1500), calls=%async_computation.3 | async-start | bytes 524288 | tf_op jit(solution)/shard_map/all_to_all | solution.py:123
  471.4 47.6 %all-to-all-start.4 = ((bf16[32,4,1024]{2,0,1:T(8,128)(2,1)}), bf16[32,4,1024]{2,0,1:T(8,128)(2,1)}, u32[]{:S(2)}, u32[]{:S(2)}) async-start(bf16[32,4,1024]{2,0,1:T(8,128)(2,1)} %bitcast.393), calls=%async_computation.4 | async-start | bytes 524288 | tf_op jit(solution)/shard_map/all_to_all | solution.py:124
  535.8 8.1 collective-permute-start.6
  538.8 8.5 collective-permute-start.7
  538.9 9.2 collective-permute-start.4
  557.3 8.7 collective-permute-start.6
  557.3 9.4 collective-permute-start.7
  558.1 9.3 collective-permute-start.4
  558.6 9.2 collective-permute-start.5
  577.1 8.4 collective-permute-start.7
  598.6 8.4 collective-permute-start.6
  598.7 9.2 collective-permute-start.7
  618.0 8.4 collective-permute-start.6
  618.1 9.2 collective-permute-start.7
  639.4 8.1 collective-permute-start.6
  639.9 8.4 collective-permute-start.7
  661.2 8.6 collective-permute-start.7
  679.9 8.9 collective-permute-start.6
  680.0 9.6 collective-permute-start.7
  699.8 8.4 collective-permute-start.6
  721.2 8.3 collective-permute-start.6
  721.9 8.4 collective-permute-start.7
  740.7 10.5 %collective-permute-start.6 = (f32[128,128]{1,0:T(8,128)S(1)}, f32[128,128]{1,0:T(8,128)}, u32[]{:S(2)}, u32[]{:S(2)}) collective-permute-start(f32[128,128]{1,0:T(8,128)S(1)} %get-tuple-element.1724), channel_id=1, source_target_pairs={{0,4},{4,8},{8,12},{12,16},{16,20},{20,24},{24,28},{28,32},{32,36}... | collective-permute-start | bytes 196616 | tf_op jit(solution)/shard_map/while/body/eval_jaxpr/ppermute | solution.py:15
  743.3 8.7 collective-permute-start.7
  764.5 8.1 collective-permute-start.6
  765.0 8.4 collective-permute-start.7
  784.2 8.1 collective-permute-start.6
  784.2 9.3 collective-permute-start.7
  803.8 8.7 collective-permute-start.6
  804.1 9.3 collective-permute-start.7
  825.4 8.1 collective-permute-start.6
  825.5 8.8 collective-permute-start.7
  845.4 9.2 collective-permute-start.6
  845.5 10.0 %collective-permute-start.7 = (f32[128,128]{1,0:T(8,128)S(1)}, f32[128,128]{1,0:T(8,128)S(1)}, u32[]{:S(2)}, u32[]{:S(2)}) collective-permute-start(f32[128,128]{1,0:T(8,128)S(1)} %get-tuple-element.1725), channel_id=1, source_target_pairs={{0,4},{4,8},{8,12},{12,16},{16,20},{20,24},{24,28},{28,32},{32,36}... | collective-permute-start | bytes 196616 | tf_op jit(solution)/shard_map/while/body/eval_jaxpr/ppermute | solution.py:15
  858.6 11.5 %all-to-all-start.5 = ((bf16[4,32,1024]{2,1,0:T(8,128)(2,1)}), bf16[4,32,1024]{2,1,0:T(8,128)(2,1)S(1)}, u32[]{:S(2)}, u32[]{:S(2)}) async-start(bf16[4,32,1024]{2,1,0:T(8,128)(2,1)} %convert_element_type.193), calls=%async_computation.5 | async-start | bytes 524288 | tf_op jit(solution)/shard_map/all_to_all | solution.py:178
  863.5 119.1 %all-gather.7.cloned.1.call-start = ((), (), s32[]{:S(2)}) async-start(), calls=%async_computation.6 | async-start | bytes 1064960 | tf_op jit(solution)/shard_map/all_gather | solution.py:216
  (84 other events, 2888.8 us)
Sparse Core Ops, SparseCore 0:
  872.9 109.6 all-gather.6
